TPU v7x, 32 devices: a whole 2x2x4 slice. The times are simulated.
32 devices in a mesh: seq: 8 (over z, y), head: 4 (over x, core).
Axes of the slice: x: 2, y: 2, z: 4, core: 2. Of those that a mesh axis runs over, the one named last changes fastest.
Arguments:
- mel_buffer: bfloat16 [16384, 128], P('seq'), may hold values from -6 to 6
- segment_frames: int32 [64], P('seq'), may hold values from 0 to 2048, as said below
- conv1_weight: bfloat16 [3, 128, 1280], replicated, may hold values from -0.3125 to 0.3125
- conv1_bias: float32 [1280], replicated, may hold values from -3 to 3
- conv2_weight: bfloat16 [3, 1280, 1280], P(None, 'seq', 'head'), may hold values from -0.09375 to 0.09375
- conv2_bias: float32 [1280], P('head'), may hold values from -3 to 3
- norm_gain: float32 [1280], replicated, may hold values from 0.1 to 1.9
- norm_bias: float32 [1280], replicated, may hold values from -3 to 3
- qkv_weight: bfloat16 [1280, 3840], P('seq', 'head'), may hold values from -0.15625 to 0.15625
Outputs:
- qkv: bfloat16 [4096, 3840], P('seq', 'head')
Inputs may be any that keep to these rules, and one draw needn't show every extreme that they name: `segment_frames`: with S_i the sum of the counts of blocks 0 to i, S_i - (i + 1) * 1024 lies in 0 to 1024 and is 0 for the last block; the counts of one block add to at most 2048, and those of some block add to exactly 2048, all of them in one segment of that block, its other segments being empty.
All inputs are finite; a program needn't handle non-finite values.
Results may differ from a plain program's by a relative error of at most 0.006.
Values may be sent and summed in bfloat16 or wider, within the bound.
A program may use at most 128 MiB of HBM per device.

v0:
```python
import functools
import math

import jax
import jax.numpy as jnp
from jax import lax
from jax.experimental import pallas as pl
from jax.experimental.pallas import tpu as pltpu
from jax.sharding import PartitionSpec as P

CONTEXT = 1500


LOG_SCALE = math.log(10000.0)


def prefix(value, axis, join, neutral):
    count, mine = (lax.axis_size(axis), lax.axis_index(axis))
    pieces = lax.all_gather(value, axis)
    running = jnp.full_like(value, 0) + jnp.asarray(neutral, value.dtype)

    def step(position, running):
        longer = join(running, pieces[position])
        return jnp.where(position < mine, longer, running)

    return lax.fori_loop(0, count - 1, step, running)


def from_behind(value, axis, by):
    size = lax.axis_size(axis)
    pairs = [(i, i + by) for i in range(size) if 0 <= i + by < size]
    return lax.ppermute(value, axis, pairs)


def padded(value, sides, width):
    for axis, dim in sides:
        size, length = (lax.axis_size(axis), value.shape[dim])
        up = [(i, (i + 1) % size) for i in range(size - 1)]
        down = [(j, i) for i, j in up]
        last = lax.slice_in_dim(value, length - width, length, axis=dim)
        initial = lax.slice_in_dim(value, 0, width, axis=dim)
        before = lax.ppermute(last, axis, up)
        after = lax.ppermute(initial, axis, down)
        value = jnp.concatenate([before, value, after], axis=dim)
    return value


def sinusoid(token_ids, channel_ids, width_all):
    half_width = width_all // 2
    inv_rate = jnp.exp(
        -(LOG_SCALE / (half_width - 1)) * (channel_ids % half_width).astype(jnp.float32)
    )
    angles = (token_ids % CONTEXT).astype(jnp.float32)[:, None] * inv_rate[None, :]
    return jnp.where(channel_ids[None, :] < half_width, jnp.sin(angles), jnp.cos(angles))


def layer_norm(values, gain, shift):
    widened = values.astype(jnp.float32)
    average = jnp.mean(widened, axis=-1, keepdims=True)
    centered = widened - average
    spread = jnp.mean(centered * centered, axis=-1, keepdims=True)
    return (centered * lax.rsqrt(spread + 1e-05) * gain + shift).astype(jnp.bfloat16)


def add_sum(left, right):
    return left + right


def project_rows(normed, shard_rows):
    return jnp.dot(normed, shard_rows, preferred_element_type=jnp.float32)


def per_device(
    mel_buffer,
    segment_frames,
    conv1_weight,
    conv1_bias,
    conv2_weight,
    conv2_bias,
    norm_gain,
    norm_bias,
    qkv_weight,
):
    frames_dev = mel_buffer.shape[0] // 2
    tok_rows = frames_dev // 2
    width_all = conv1_weight.shape[2]
    seq_place = lax.axis_index("seq")
    head_place = lax.axis_index("head")
    own_count = jnp.sum(segment_frames)
    start_frame = prefix(own_count, "seq", add_sum, jnp.zeros((), jnp.int32))
    displaced = (start_frame - seq_place * frames_dev).astype(jnp.int32)
    tail_rows = lax.dynamic_slice_in_dim(mel_buffer, frames_dev - displaced, frames_dev, 0)
    arrived = from_behind(tail_rows, "seq", 1)
    front_pad = jnp.concatenate([jnp.zeros_like(arrived), mel_buffer[:frames_dev]], axis=0)
    own_rows = lax.dynamic_slice_in_dim(front_pad, frames_dev - displaced, frames_dev, 0)
    row_ids = jnp.arange(frames_dev, dtype=jnp.int32)
    frames = jnp.where((row_ids < displaced)[:, None], arrived, own_rows)
    rimmed = padded(frames, (("seq", 0),), 2)
    running = jnp.zeros((frames_dev + 1, width_all), jnp.float32)
    for k in range(3):
        running = running + jnp.dot(
            rimmed[k : k + frames_dev + 1], conv1_weight[k], preferred_element_type=jnp.float32
        )
    first_layer = jax.nn.gelu(running + conv1_bias, approximate=False).astype(jnp.bfloat16)
    keep_mask = (jnp.arange(frames_dev + 1, dtype=jnp.int32) > 0) | (seq_place > 0)
    first_layer = jnp.where(keep_mask[:, None], first_layer, jnp.zeros_like(first_layer))
    frame_pairs = first_layer[:frames_dev].reshape(tok_rows, 2, width_all)
    later_pairs = first_layer[1:].reshape(tok_rows, 2, width_all)
    conv_taps = (frame_pairs[:, 0], frame_pairs[:, 1], later_pairs[:, 1])
    quarter_width = conv2_weight.shape[2]
    zero_start = jnp.zeros((tok_rows, quarter_width), jnp.float32)
    stem_sum = zero_start
    shard_rows = lax.all_gather(conv2_weight, "seq", axis=1, tiled=True)
    for k in range(3):
        inputs = conv_taps[k]
        stem_sum = stem_sum + jnp.dot(inputs, shard_rows[k], preferred_element_type=jnp.float32)
    token_ids = seq_place * tok_rows + jnp.arange(tok_rows, dtype=jnp.int32)
    channel = head_place * quarter_width + jnp.arange(quarter_width, dtype=jnp.int32)
    features = (
        jax.nn.gelu(stem_sum + conv2_bias, approximate=False)
        + sinusoid(token_ids, channel, width_all)
    ).astype(jnp.bfloat16)
    quarter = lax.all_to_all(features, "head", split_axis=0, concat_axis=1, tiled=True)
    normed = layer_norm(quarter, norm_gain, norm_bias)
    widened_rows = lax.all_gather(qkv_weight, "head", axis=1, tiled=True)
    qkv_part = project_rows(normed, lax.all_gather(widened_rows, "seq", axis=0, tiled=True))
    return lax.all_to_all(
        qkv_part.astype(jnp.bfloat16), "head", split_axis=1, concat_axis=0, tiled=True
    )


MESH = pl.DeviceIdType.MESH
HALO = 16
Y_FIRST = (2,)


def gelu(v):
    return 0.5 * v * (1.0 + lax.erf(v * math.sqrt(0.5)))


def fused_kernel(
    dims, vec_ref, mel_ref, w1_ref, w2_ref, wq_ref,
    out_ref, seg_all, tail_send, tail_recv, fr, halo_prev, halo_next, ebuf, obuf, x_even, x_odd,
    f_even, f_odd, w2g, wqg, rest, restg, stem, acc0, seg_s, seg_r, tail_s, tail_r, halo_s, halo_r,
    w_s, w_r, loc, st_s, st_r,
):
    n, depth, width_all, quarter = dims
    nz = n // 2
    toks = fr.shape[1]
    frames_dev = 2 * toks
    me = lax.axis_index("seq")
    h = lax.axis_index("head")
    z, y = me // 2, me % 2
    partner = z * 2 + (1 - y)
    f32, bf16 = jnp.float32, jnp.bfloat16
    core = h % 2
    core_peer = (h // 2) * 2 + (1 - core)
    seg_ref = vec_ref.at[pl.ds(8, 8), pl.ds(0, 128)]
    pending = []

    def remote(src, dst, ss, rs, axis, peer):
        return pltpu.make_async_remote_copy(
            src_ref=src, dst_ref=dst, send_sem=ss, recv_sem=rs,
            device_id={axis: peer}, device_id_type=MESH,
        )

    def start(cond, copy):
        if cond is None:
            copy.start()
        else:
            pl.when(cond)(copy.start)
        pending.append((cond, copy))

    def both(a, b):
        if a is None:
            return b
        return a if b is None else jnp.logical_and(a, b)

    barrier = pltpu.get_barrier_semaphore()
    for p in range(1, n):
        pl.semaphore_signal(
            barrier, inc=1, device_id={"seq": lax.rem(me + p, n)}, device_id_type=MESH
        )
    for p in range(1, 4):
        pl.semaphore_signal(
            barrier, inc=1, device_id={"head": lax.rem(h + p, 4)}, device_id_type=MESH
        )
    pl.semaphore_wait(barrier, n - 1 + 3)

    for p in range(1, n):
        dst = lax.rem(me + p, n)
        start(None, remote(seg_ref, seg_all.at[me], seg_s.at[p], seg_r.at[me], "seq", dst))

    half = depth // 2
    out_cols = wqg.shape[1]
    main2, main_q = quarter - 64, out_cols - 64
    lanes2, lanes_q = pl.ds(0, main2), pl.ds(0, main_q)

    def gathered(p, s):
        if p < 3:
            return w2g.at[p, pl.ds(pl.multiple_of(s * depth, 16), depth), lanes2]
        if p == 5:
            return restg.at[s]
        return wqg.at[pl.ds(pl.multiple_of(s * depth + (p - 3) * half, 16), half), lanes_q]

    def own(p):
        if p == 5:
            return rest
        return w2_ref.at[p, :, lanes2] if p < 3 else wq_ref.at[pl.ds((p - 3) * half, half), lanes_q]

    has_up, has_down = z < nz - 1, z > 0

    def push(cond, p, s, way, mine=False):
        peer = (lax.rem(me + 2, n), lax.rem(me + n - 2, n), partner)[way]
        src = own(p) if mine else gathered(p, s)
        start(cond, remote(src, gathered(p, s), w_s.at[p, s, way], w_r.at[p, s], "seq", peer))

    def arrive(cond, p, s):
        copy = remote(gathered(p, s), gathered(p, s), w_s.at[p, s, 0], w_r.at[p, s], "seq", partner)
        if cond is None:
            copy.wait_recv()
        else:
            pl.when(cond)(copy.wait_recv)

    def start_own(p):
        push(None, p, me, 2, True)
        push(has_up, p, me, 0, True)
        push(has_down, p, me, 1, True)
        pltpu.make_async_copy(own(p), gathered(p, me), loc.at[p]).start()

    def relay_partner(p):
        if p in Y_FIRST:
            arrive(None, p, partner)
            push(has_up, p, partner, 0)
            push(has_down, p, partner, 1)

    def relay(p, k):
        for way in (0, 1):
            valid = z - k >= 0 if way == 0 else z + k <= nz - 1
            onward = has_up if way == 0 else has_down
            shift = -2 * k if way == 0 else 2 * k
            for base in (me, partner) if p in Y_FIRST else (me,):
                s = lax.rem(base + shift + 2 * n, n)
                arrive(valid, p, s)
                push(both(valid, onward), p, s, way)
                if p not in Y_FIRST:
                    push(valid, p, s, 2)

    def finish(p):
        if p not in Y_FIRST:
            for q in range(nz):
                arrive(None, p, 2 * q + (1 - y))
        pltpu.make_async_copy(own(p), gathered(p, me), loc.at[p]).wait()

    early = (2, 5, 0, 1)
    start_own(2)
    rest[0:depth, 0:64] = w2_ref[0, :, main2:]
    rest[0:depth, 64:128] = w2_ref[1, :, main2:]
    rest[depth : depth + half, 0:64] = w2_ref[2, 0:half, main2:]
    rest[depth : depth + half, 64:128] = w2_ref[2, half:, main2:]
    rest[depth + half :, 0:64] = wq_ref[0:half, main_q:]
    rest[depth + half :, 64:128] = wq_ref[half:, main_q:]
    for p in early[1:]:
        start_own(p)

    total = jnp.zeros((8, 128), f32)
    for p in range(1, n):
        src = lax.rem(me + n - p, n)
        remote(seg_ref, seg_all.at[src], seg_s.at[p], seg_r.at[src], "seq", src).wait_recv()
        total = total + jnp.where(src < me, seg_all[src], 0.0)
    total = jnp.sum(jnp.sum(total, axis=1, keepdims=True), axis=0, keepdims=True)
    moved = total.astype(jnp.int32) - me * frames_dev

    rows = 128

    def shifted(first, parity, depth_rows):
        frame = 2 * (first + lax.broadcasted_iota(jnp.int32, (rows, depth_rows), 0)) + parity
        column = lax.broadcasted_iota(jnp.int32, (rows, depth_rows), 1)
        pick = jnp.where(frame - column == moved, 1.0, 0.0).astype(bf16)
        return jnp.dot(pick, mel_ref[:depth_rows, :], preferred_element_type=f32)

    def tail_step(i, c):
        at = pl.multiple_of(i * rows, rows)
        tail_send[pl.ds(at, rows), :] = shifted(toks + at, core, 2 * frames_dev).astype(bf16)
        return c

    lax.fori_loop(0, toks // rows, tail_step, 0)
    tail = remote(tail_send, tail_recv.at[core], tail_s.at[0], tail_r.at[core],
                  "seq", lax.rem(me + 1, n))
    start(me < n - 1, tail)

    relay_partner(2)

    for parity, buf in ((0, ebuf), (1, obuf)):
        def own_step(i, c):
            at = pl.multiple_of(i * rows, rows)
            buf[pl.ds(HALO + at, rows), :] = shifted(at, parity, frames_dev)
            return c
        lax.fori_loop(0, toks // rows, own_step, 0)

    pl.when(me > 0)(tail.wait_recv)
    start(me > 0, remote(tail_recv.at[core], tail_recv.at[core], tail_s.at[1], tail_r.at[core],
                         "head", core_peer))
    pl.when(me > 0)(remote(
        tail_recv.at[1 - core], tail_recv.at[1 - core], tail_s.at[1], tail_r.at[1 - core],
        "head", core_peer).wait_recv)
    for parity, buf in ((0, ebuf), (1, obuf)):
        frame = 2 * lax.broadcasted_iota(jnp.int32, (toks, 128), 0) + parity
        joined = jnp.where(
            frame < moved, tail_recv[parity].astype(f32), buf[HALO : HALO + toks, :])
        buf[HALO : HALO + toks, :] = joined
        fr[parity] = joined.astype(bf16)

    nxt, prv = lax.rem(me + 1, n), lax.rem(me + n - 1, n)
    halos = [
        (me < n - 1, me > 0, fr.at[0, pl.ds(toks - HALO, HALO), :], halo_prev.at[0], nxt),
        (me < n - 1, me > 0, fr.at[1, pl.ds(toks - HALO, HALO), :], halo_prev.at[1], nxt),
        (me > 0, me < n - 1, fr.at[0, pl.ds(0, HALO), :], halo_next, prv),
    ]
    copies = [remote(s, d, halo_s.at[i], halo_r.at[i], "seq", peer)
              for i, (_, _, s, d, peer) in enumerate(halos)]
    for (sends, _, _, _, _), copy in zip(halos, copies):
        start(sends, copy)

    for p in early:
        relay(p, 1)

    x_even[:, 128:256] = fr[0]
    x_even[:, 256:384] = fr[1]

    for (_, takes, _, _, _), copy in zip(halos, copies):
        pl.when(takes)(copy.wait_recv)
    ebuf[0:HALO, :] = jnp.where(me > 0, halo_prev[0].astype(f32), 0.0)
    obuf[0:HALO, :] = jnp.where(me > 0, halo_prev[1].astype(f32), 0.0)
    ebuf[HALO + toks :, :] = jnp.where(me < n - 1, halo_next[...].astype(f32), 0.0)
    x_even[:, 0:128] = obuf[HALO - 1 : HALO - 1 + toks, :].astype(bf16)
    x_odd[:, 0:128] = ebuf[0 : HALO + toks, :].astype(bf16)
    x_odd[:, 128:256] = obuf[0 : HALO + toks, :].astype(bf16)
    x_odd[:, 256:384] = ebuf[1 : HALO + toks + 1, :].astype(bf16)

    start_own(3)
    start_own(4)

    cols = 256

    def even_step(i, c):
        at = pl.ds(pl.multiple_of(i * cols, cols), cols)
        acc = jnp.dot(x_even[...], w1_ref[:, at], preferred_element_type=f32)
        f_even[:, at] = gelu(acc + vec_ref[0:1, at]).astype(bf16)
        return c

    def odd_step(i, c):
        at = pl.ds(pl.multiple_of(i * cols, cols), cols)
        acc = jnp.dot(x_odd[...], w1_ref[:, at], preferred_element_type=f32)
        f_odd[:, at] = gelu(acc + vec_ref[0:1, at]).astype(bf16)
        return c

    lax.fori_loop(0, width_all // cols, even_step, 0)
    for p in early:
        relay(p, 2)
    lax.fori_loop(0, width_all // cols, odd_step, 0)
    keep = jnp.where(me > 0, f_odd[0:HALO, :].astype(f32), 0.0)
    f_odd[0:HALO, :] = keep.astype(bf16)
    for p in (3, 4):
        relay(p, 1)
    for p in early:
        for k in range(3, nz):
            relay(p, k)
    for p in (3, 4):
        relay(p, 2)
    for p in early:
        finish(p)

    for j in range(n):
        at = slice(j * depth, (j + 1) * depth)
        w2g[0, at, main2:] = restg[j, 0:depth, 0:64]
        w2g[1, at, main2:] = restg[j, 0:depth, 64:128]
        w2g[2, j * depth : j * depth + half, main2:] = restg[j, depth : depth + half, 0:64]
        w2g[2, j * depth + half : (j + 1) * depth, main2:] = restg[j, depth : depth + half, 64:128]
        wqg[j * depth : j * depth + half, main_q:] = restg[j, depth + half :, 0:64]
        wqg[j * depth + half : (j + 1) * depth, main_q:] = restg[j, depth + half :, 64:128]

    odd_rows = (HALO + toks) // 3

    def tap_zero(i, c):
        at = pl.ds(pl.multiple_of(i * odd_rows, 16), odd_rows)
        acc0[at, :] = jnp.dot(f_odd[at, :], w2g[0], preferred_element_type=f32)
        return c

    lax.fori_loop(0, 3, tap_zero, 0)
    half_width = width_all // 2
    lane = lax.broadcasted_iota(jnp.int32, (1, quarter), 1) + lax.rem(h * quarter, half_width)
    rate = jnp.exp(-(LOG_SCALE / (half_width - 1)) * lane.astype(f32))
    first_token = lax.rem(me * toks, CONTEXT)
    for i in range(toks // rows):
        acc = jnp.dot(f_even[i * rows : (i + 1) * rows, :], w2g[1], preferred_element_type=f32)
        acc = acc + jnp.dot(
            f_odd[HALO + i * rows : HALO + (i + 1) * rows, :], w2g[2], preferred_element_type=f32)
        acc = acc + acc0[HALO - 1 + i * rows : HALO - 1 + (i + 1) * rows, :]
        token = first_token + i * rows + lax.broadcasted_iota(jnp.int32, (rows, 1), 0)
        token = jnp.where(token >= CONTEXT, token - CONTEXT, token)
        angle = token.astype(f32) * rate
        place = jnp.where(h * quarter < half_width, jnp.sin(angle), jnp.cos(angle))
        stem[h, i * rows : (i + 1) * rows, :] = (gelu(acc + vec_ref[3:4, 0:quarter]) + place).astype(bf16)

    x_peer = lax.rem(h + 2, 4)
    far = lax.rem(core_peer + 2, 4)
    start(None, remote(stem.at[h], stem.at[h], st_s.at[0], st_r.at[0], "head", x_peer))
    start(None, remote(stem.at[h], stem.at[h], st_s.at[1], st_r.at[1], "head", core_peer))
    for p in (3, 4):
        for k in range(3, nz):
            relay(p, k)
    remote(stem.at[x_peer], stem.at[x_peer], st_s.at[0], st_r.at[0], "head", x_peer).wait_recv()
    start(None, remote(stem.at[x_peer], stem.at[x_peer], st_s.at[2], st_r.at[2], "head", core_peer))
    remote(stem.at[core_peer], stem.at[core_peer], st_s.at[1], st_r.at[1], "head", core_peer).wait_recv()
    remote(stem.at[far], stem.at[far], st_s.at[2], st_r.at[2], "head", core_peer).wait_recv()
    for p in (3, 4):
        finish(p)

    def project(i, c):
        at = pl.ds(pl.multiple_of(i * rows, rows), rows)
        parts = [stem[j, at, :].astype(f32) for j in range(4)]
        mean = sum(jnp.sum(v, axis=1, keepdims=True) for v in parts) / width_all
        parts = [v - mean for v in parts]
        var = sum(jnp.sum(v * v, axis=1, keepdims=True) for v in parts) / width_all
        scale = lax.rsqrt(var + 1e-05)
        acc = None
        for j in range(4):
            lanes = slice(j * quarter, (j + 1) * quarter)
            normed = (parts[j] * scale * vec_ref[1:2, lanes] + vec_ref[2:3, lanes]).astype(bf16)
            term = jnp.dot(normed, wqg[lanes, :], preferred_element_type=f32)
            acc = term if acc is None else acc + term
        out_ref[at, :] = acc.astype(bf16)
        return c

    lax.fori_loop(0, toks // rows, project, 0)

    for cond, copy in pending:
        if cond is None:
            copy.wait_send()
        else:
            pl.when(cond)(copy.wait_send)


def fused_device(
    n, mel_buffer, segment_frames, conv1_weight, conv1_bias, conv2_weight, conv2_bias,
    norm_gain, norm_bias, qkv_weight,
):
    toks = mel_buffer.shape[0] // 4
    taps, mels, width_all = conv1_weight.shape
    depth, quarter = conv2_weight.shape[1:]
    out_cols = qkv_weight.shape[1]
    bf16, f32 = jnp.bfloat16, jnp.float32
    vec = jnp.zeros((), f32)
    rows_of = (conv1_bias, norm_gain, norm_bias, conv2_bias), (segment_frames.astype(f32),)
    for first, group in zip((0, 8), rows_of):
        for j, row in enumerate(group):
            vec = vec + jnp.pad(row[None, :], ((first + j, 15 - first - j), (0, width_all - row.shape[0])))
    vmem = pl.BlockSpec(memory_space=pltpu.VMEM)
    dma = pltpu.SemaphoreType.DMA
    return pl.pallas_call(
        functools.partial(fused_kernel, (n, depth, width_all, quarter)),
        out_shape=jax.ShapeDtypeStruct((toks, out_cols), bf16),
        in_specs=[vmem] * 5,
        out_specs=vmem,
        scratch_shapes=[
            pltpu.VMEM((n, 8, 128), f32),
            pltpu.VMEM((toks, 128), bf16),
            pltpu.VMEM((2, toks, 128), bf16),
            pltpu.VMEM((2, toks, 128), bf16),
            pltpu.VMEM((2, HALO, 128), bf16),
            pltpu.VMEM((HALO, 128), bf16),
            pltpu.VMEM((toks + 2 * HALO, 128), f32),
            pltpu.VMEM((toks + 2 * HALO, 128), f32),
            pltpu.VMEM((toks, 384), bf16),
            pltpu.VMEM((toks + HALO, 384), bf16),
            pltpu.VMEM((toks, width_all), bf16),
            pltpu.VMEM((toks + HALO, width_all), bf16),
            pltpu.VMEM((3, width_all, quarter), bf16),
            pltpu.VMEM((width_all, out_cols), bf16),
            pltpu.VMEM((2 * depth, 128), bf16),
            pltpu.VMEM((n, 2 * depth, 128), bf16),
            pltpu.VMEM((4, toks, quarter), bf16),
            pltpu.VMEM((toks + HALO, quarter), f32),
            dma((n,)), dma((n,)), dma((2,)), dma((2,)), dma((3,)), dma((3,)),
            dma((6, n, 3)), dma((6, n)), dma((6,)), dma((3,)), dma((3,)),
        ],
        compiler_params=pltpu.CompilerParams(
            collective_id=0, has_side_effects=True, vmem_limit_bytes=60 * 1024 * 1024
        ),
    )(
        vec, mel_buffer, conv1_weight.reshape(taps * mels, width_all), conv2_weight, qkv_weight,
    )


def solution(mesh):
    n_seq, n_head = mesh.shape["seq"], mesh.shape["head"]

    def local(*args):
        depth = args[4].shape[1]
        if n_head == 4 and n_seq % 2 == 0 and depth % 32 == 0 and args[4].shape[2] % 128 == 64:
            return fused_device(n_seq, *args)
        return per_device(*args)

    in_specs = (
        P("seq", None),
        P("seq"),
        P(),
        P(),
        P(None, "seq", "head"),
        P("head"),
        P(),
        P(),
        P("seq", "head"),
    )
    out_specs = P("seq", "head")
    return jax.shard_map(
        local, mesh=mesh, in_specs=in_specs, out_specs=out_specs, check_vma=False
    )
```

profile of v0, /device:TPU:0, one launch (start us, length us, event | category | flops | bytes accessed | tf_op | source)
XLA Modules:
  0.0 82.6 jit_solution(103325529234359585)
XLA Ops:
  0.0 0.0 copy-start.2
  0.0 0.7 convert_bitcast_fusion
  0.7 0.0 copy-done.2
  0.7 0.0 copy-start
  0.7 0.7 broadcast_in_dim.15
  1.4 0.0 copy-done
  1.4 0.0 copy-start.1
  1.4 0.7 copy-done.1
  2.1 0.7 pad_add_fusion.vec_ref
  2.8 77.6 %shard_map.91 = bf16[512,960]{1,0:T(8,128)(2,1)} custom-call(f32[16,1280]{1,0:T(8,128)} %pad_add_fusion.vec_ref, bf16[2048,128]{1,0:T(8,128)(2,1)} %mel_ref.1, bf16[384,1280]{1,0:T(8,128)(2,1)} %bitcast.3, bf16[3,160,320]{2,1,0:T(8,128)(2,1)} %w2_ref.1, bf16[160,960]{1,0:T(8,128)(2,1)} %wq_ref.1), custom_call_target="tpu_custom_call" | custom-call | tf_op jit(solution)/shard_map/pallas_call | solution.py:461
  80.3 2.2 %copy.10 = bf16[512,960]{0,1:T(8,128)(2,1)} copy(bf16[512,960]{1,0:T(8,128)(2,1)} %shard_map.91) | data formatting | bytes 1966080 | tf_op jit(solution)/shard_map/pallas_call | solution.py:461
  (3 shorter events, 0.0 us)
Async XLA Ops:
  0.0 0.7 copy-start.2
  0.7 0.7 copy-start
  1.4 0.7 copy-start.1
where the time goes:
time: 82.9 us; the launch traced here: 82.6 us
  Pallas kernels  77.6 us (94%)
  local copies, waits for them, and re-layouts  3.67 us (4%)
  other arithmetic  1.33 us (2%)
    pallas_call x1, Pallas kernels, fused_device(): pl.pallas_call(functools.partial(fused_kernel, (n, depth, width_all, quar...  77.6 us
    pallas_call x1, local copies, waits for them, and re-layouts, fused_device(): pl.pallas_call(functools.partial(fused_kernel, (n, depth, width_all, quar...  2.25 us

commit v1 on v0

v1 whole, which is shorter than its diff:
```python
import functools
import math

import jax
import jax.numpy as jnp
from jax import lax
from jax.experimental import pallas as pl
from jax.experimental.pallas import tpu as pltpu
from jax.sharding import PartitionSpec as P

CONTEXT = 1500


LOG_SCALE = math.log(10000.0)


def prefix(value, axis, join, neutral):
    count, mine = (lax.axis_size(axis), lax.axis_index(axis))
    pieces = lax.all_gather(value, axis)
    running = jnp.full_like(value, 0) + jnp.asarray(neutral, value.dtype)

    def step(position, running):
        longer = join(running, pieces[position])
        return jnp.where(position < mine, longer, running)

    return lax.fori_loop(0, count - 1, step, running)


def from_behind(value, axis, by):
    size = lax.axis_size(axis)
    pairs = [(i, i + by) for i in range(size) if 0 <= i + by < size]
    return lax.ppermute(value, axis, pairs)


def padded(value, sides, width):
    for axis, dim in sides:
        size, length = (lax.axis_size(axis), value.shape[dim])
        up = [(i, (i + 1) % size) for i in range(size - 1)]
        down = [(j, i) for i, j in up]
        last = lax.slice_in_dim(value, length - width, length, axis=dim)
        initial = lax.slice_in_dim(value, 0, width, axis=dim)
        before = lax.ppermute(last, axis, up)
        after = lax.ppermute(initial, axis, down)
        value = jnp.concatenate([before, value, after], axis=dim)
    return value


def sinusoid(token_ids, channel_ids, width_all):
    half_width = width_all // 2
    inv_rate = jnp.exp(
        -(LOG_SCALE / (half_width - 1)) * (channel_ids % half_width).astype(jnp.float32)
    )
    angles = (token_ids % CONTEXT).astype(jnp.float32)[:, None] * inv_rate[None, :]
    return jnp.where(channel_ids[None, :] < half_width, jnp.sin(angles), jnp.cos(angles))


def layer_norm(values, gain, shift):
    widened = values.astype(jnp.float32)
    average = jnp.mean(widened, axis=-1, keepdims=True)
    centered = widened - average
    spread = jnp.mean(centered * centered, axis=-1, keepdims=True)
    return (centered * lax.rsqrt(spread + 1e-05) * gain + shift).astype(jnp.bfloat16)


def add_sum(left, right):
    return left + right


def project_rows(normed, shard_rows):
    return jnp.dot(normed, shard_rows, preferred_element_type=jnp.float32)


def per_device(
    mel_buffer,
    segment_frames,
    conv1_weight,
    conv1_bias,
    conv2_weight,
    conv2_bias,
    norm_gain,
    norm_bias,
    qkv_weight,
):
    frames_dev = mel_buffer.shape[0] // 2
    tok_rows = frames_dev // 2
    width_all = conv1_weight.shape[2]
    seq_place = lax.axis_index("seq")
    head_place = lax.axis_index("head")
    own_count = jnp.sum(segment_frames)
    start_frame = prefix(own_count, "seq", add_sum, jnp.zeros((), jnp.int32))
    displaced = (start_frame - seq_place * frames_dev).astype(jnp.int32)
    tail_rows = lax.dynamic_slice_in_dim(mel_buffer, frames_dev - displaced, frames_dev, 0)
    arrived = from_behind(tail_rows, "seq", 1)
    front_pad = jnp.concatenate([jnp.zeros_like(arrived), mel_buffer[:frames_dev]], axis=0)
    own_rows = lax.dynamic_slice_in_dim(front_pad, frames_dev - displaced, frames_dev, 0)
    row_ids = jnp.arange(frames_dev, dtype=jnp.int32)
    frames = jnp.where((row_ids < displaced)[:, None], arrived, own_rows)
    rimmed = padded(frames, (("seq", 0),), 2)
    running = jnp.zeros((frames_dev + 1, width_all), jnp.float32)
    for k in range(3):
        running = running + jnp.dot(
            rimmed[k : k + frames_dev + 1], conv1_weight[k], preferred_element_type=jnp.float32
        )
    first_layer = jax.nn.gelu(running + conv1_bias, approximate=False).astype(jnp.bfloat16)
    keep_mask = (jnp.arange(frames_dev + 1, dtype=jnp.int32) > 0) | (seq_place > 0)
    first_layer = jnp.where(keep_mask[:, None], first_layer, jnp.zeros_like(first_layer))
    frame_pairs = first_layer[:frames_dev].reshape(tok_rows, 2, width_all)
    later_pairs = first_layer[1:].reshape(tok_rows, 2, width_all)
    conv_taps = (frame_pairs[:, 0], frame_pairs[:, 1], later_pairs[:, 1])
    quarter_width = conv2_weight.shape[2]
    zero_start = jnp.zeros((tok_rows, quarter_width), jnp.float32)
    stem_sum = zero_start
    shard_rows = lax.all_gather(conv2_weight, "seq", axis=1, tiled=True)
    for k in range(3):
        inputs = conv_taps[k]
        stem_sum = stem_sum + jnp.dot(inputs, shard_rows[k], preferred_element_type=jnp.float32)
    token_ids = seq_place * tok_rows + jnp.arange(tok_rows, dtype=jnp.int32)
    channel = head_place * quarter_width + jnp.arange(quarter_width, dtype=jnp.int32)
    features = (
        jax.nn.gelu(stem_sum + conv2_bias, approximate=False)
        + sinusoid(token_ids, channel, width_all)
    ).astype(jnp.bfloat16)
    quarter = lax.all_to_all(features, "head", split_axis=0, concat_axis=1, tiled=True)
    normed = layer_norm(quarter, norm_gain, norm_bias)
    widened_rows = lax.all_gather(qkv_weight, "head", axis=1, tiled=True)
    qkv_part = project_rows(normed, lax.all_gather(widened_rows, "seq", axis=0, tiled=True))
    return lax.all_to_all(
        qkv_part.astype(jnp.bfloat16), "head", split_axis=1, concat_axis=0, tiled=True
    )


MESH = pl.DeviceIdType.MESH
HALO = 16
ROWS = 128
W2_PIECES = (2, 0, 1, 5)
WQ_PIECES = (3, 4, 6)


def gelu(v):
    return 0.5 * v * (1.0 + lax.erf(v * math.sqrt(0.5)))


def fused_kernel(
    dims, vec_ref, mel_ref, w1_ref, w2_ref, wq_ref,
    out_ref, seg_all, tail_send, tail_recv, fr, frp, halo_prev, halo_next, ebuf, obuf, x_even, x_odd,
    w1h, b1h, f_mid, f_odd, w2g, wqg, rest, restg, restq, restqg, acc0, accp, psend, precv, place,
    stem, gperm, nrm, seg_s, seg_r, tail_s, tail_r, fr_s, fr_r, halo_s, halo_r,
    w_s, w_r, loc, p_s, p_r, st_s, st_r,
):
    n, depth, width_all, quarter = dims
    nz = n // 2
    toks = fr.shape[1]
    frames_dev = 2 * toks
    plane = 2 * toks
    half_width = width_all // 2
    chunks = toks // ROWS
    me = lax.axis_index("seq")
    h = lax.axis_index("head")
    z, y = me // 2, me % 2
    partner = z * 2 + (1 - y)
    f32, bf16 = jnp.float32, jnp.bfloat16
    core = h % 2
    core_peer = (h // 2) * 2 + (1 - core)
    x_peer = lax.rem(h + 2, 4)
    far = lax.rem(core_peer + 2, 4)
    seg_ref = vec_ref.at[pl.ds(8, 8), pl.ds(0, 128)]
    pending = []

    def remote(src, dst, ss, rs, axis, peer):
        return pltpu.make_async_remote_copy(
            src_ref=src, dst_ref=dst, send_sem=ss, recv_sem=rs,
            device_id={axis: peer}, device_id_type=MESH,
        )

    def start(cond, copy):
        if cond is None:
            copy.start()
        else:
            pl.when(cond)(copy.start)
        pending.append((cond, copy))

    def both(a, b):
        if a is None:
            return b
        return a if b is None else jnp.logical_and(a, b)

    barrier = pltpu.get_barrier_semaphore()
    for p in range(1, n):
        pl.semaphore_signal(
            barrier, inc=1, device_id={"seq": lax.rem(me + p, n)}, device_id_type=MESH
        )
    for p in range(1, 4):
        pl.semaphore_signal(
            barrier, inc=1, device_id={"head": lax.rem(h + p, 4)}, device_id_type=MESH
        )
    pl.semaphore_wait(barrier, n - 1 + 3)

    for p in range(1, n):
        dst = lax.rem(me + p, n)
        start(None, remote(seg_ref, seg_all.at[me], seg_s.at[p], seg_r.at[me], "seq", dst))

    half = depth // 2
    out_cols = wqg.shape[1]
    main2, main_q = quarter - 64, out_cols - 64
    head_rows = 2 * depth - 64
    first_q = head_rows - depth
    lanes2, lanes_q = pl.ds(0, main2), pl.ds(0, main_q)
    rest_base = 4 * head_rows

    def row_first(s):
        return (s // 2) * head_rows + (s % 2) * depth

    def row_last(s):
        even = (s // 2) * head_rows + first_q
        odd = rest_base + (s // 2) * 64
        return (1 - s % 2) * even + (s % 2) * odd

    def gathered(p, s):
        if p < 3:
            return w2g.at[pl.ds(pl.multiple_of(p * half_width + (s // 2) * depth, 32), depth), lanes2]
        if p == 5:
            return restg.at[s // 2]
        if p == 6:
            return restqg.at[s]
        if p == 3:
            return wqg.at[pl.ds(pl.multiple_of(row_first(s), 32), first_q), lanes_q]
        return wqg.at[pl.ds(pl.multiple_of(row_last(s), 32), 64), lanes_q]

    def own(p):
        if p < 3:
            return w2_ref.at[p, :, lanes2]
        if p == 5:
            return rest
        if p == 6:
            return restq
        return wq_ref.at[pl.ds(0, first_q) if p == 3 else pl.ds(first_q, 64), lanes_q]

    has_up, has_down = z < nz - 1, z > 0

    def push(cond, p, s, way, mine=False):
        peer = (lax.rem(me + 2, n), lax.rem(me + n - 2, n), partner)[way]
        src = own(p) if mine else gathered(p, s)
        start(cond, remote(src, gathered(p, s), w_s.at[p, s, way], w_r.at[p, s], "seq", peer))

    def arrive(cond, p, s):
        copy = remote(gathered(p, s), gathered(p, s), w_s.at[p, s, 0], w_r.at[p, s], "seq", partner)
        if cond is None:
            copy.wait_recv()
        else:
            pl.when(cond)(copy.wait_recv)

    def own_along_z(p):
        push(has_up, p, me, 0, True)
        push(has_down, p, me, 1, True)

    def own_local(p):
        return pltpu.make_async_copy(own(p), gathered(p, me), loc.at[p])

    def source(k, way):
        valid = z - k >= 0 if way == 0 else z + k <= nz - 1
        onward = has_up if way == 0 else has_down
        s = lax.rem(me + (-2 * k if way == 0 else 2 * k) + 2 * n, n)
        return valid, onward, s

    def relay(p, k):
        for way in (0, 1):
            valid, onward, s = source(k, way)
            arrive(valid, p, s)
            push(both(valid, onward), p, s, way)

    def relay_z(p, k):
        for way in (0, 1):
            valid, onward, s = source(k, way)
            arrive(both(valid, onward), p, s)
            push(both(valid, onward), p, s, way)

    def relay_y(p, k):
        for way in (0, 1):
            valid, onward, s = source(k, way)
            arrive(both(valid, jnp.logical_not(onward)), p, s)
            push(valid, p, s, 2)

    own_along_z(2)
    own_along_z(0)
    restq[:, 0:64] = wq_ref[0:half, main_q:]
    restq[:, 64:128] = wq_ref[half:, main_q:]
    rest[0:depth, 0:64] = w2_ref[0, :, main2:]
    rest[0:depth, 64:128] = w2_ref[1, :, main2:]
    rest[depth:, 0:64] = w2_ref[2, 0:half, main2:]
    rest[depth:, 64:128] = w2_ref[2, half:, main2:]
    for p in W2_PIECES + WQ_PIECES:
        own_local(p).start()

    total = jnp.zeros((8, 128), f32)
    for p in range(1, n):
        src = lax.rem(me + n - p, n)
        remote(seg_ref, seg_all.at[src], seg_s.at[p], seg_r.at[src], "seq", src).wait_recv()
        total = total + jnp.where(src < me, seg_all[src], 0.0)
    total = jnp.sum(jnp.sum(total, axis=1, keepdims=True), axis=0, keepdims=True)
    moved = total.astype(jnp.int32) - me * frames_dev

    rows = ROWS

    def shifted(first, parity, depth_rows):
        frame = 2 * (first + lax.broadcasted_iota(jnp.int32, (rows, depth_rows), 0)) + parity
        column = lax.broadcasted_iota(jnp.int32, (rows, depth_rows), 1)
        pick = jnp.where(frame - column == moved, 1.0, 0.0).astype(bf16)
        return jnp.dot(pick, mel_ref[:depth_rows, :], preferred_element_type=f32)

    def tail_step(i, c):
        at = pl.multiple_of(i * rows, rows)
        tail_send[pl.ds(at, rows), :] = shifted(toks + at, core, 2 * frames_dev).astype(bf16)
        return c

    lax.fori_loop(0, toks // rows, tail_step, 0)
    tail = remote(tail_send, tail_recv.at[core], tail_s.at[0], tail_r.at[core],
                  "seq", lax.rem(me + 1, n))
    start(me < n - 1, tail)
    own_along_z(1)
    own_along_z(5)

    base = pl.multiple_of(HALO + y * toks, 16)
    other = pl.multiple_of(HALO + (1 - y) * toks, 16)
    for parity, buf in ((0, ebuf), (1, obuf)):
        def own_step(i, c):
            at = pl.multiple_of(i * rows, rows)
            buf[pl.ds(base + at, rows), :] = shifted(at, parity, frames_dev)
            return c
        lax.fori_loop(0, toks // rows, own_step, 0)
    for p in W2_PIECES[:2]:
        relay(p, 1)

    pl.when(me > 0)(tail.wait_recv)
    start(me > 0, remote(tail_recv.at[core], tail_recv.at[core], tail_s.at[1], tail_r.at[core],
                         "head", core_peer))
    pl.when(me > 0)(remote(
        tail_recv.at[1 - core], tail_recv.at[1 - core], tail_s.at[1], tail_r.at[1 - core],
        "head", core_peer).wait_recv)
    for parity, buf in ((0, ebuf), (1, obuf)):
        frame = 2 * lax.broadcasted_iota(jnp.int32, (toks, 128), 0) + parity
        joined = jnp.where(
            frame < moved, tail_recv[parity].astype(f32), buf[pl.ds(base, toks), :])
        buf[pl.ds(base, toks), :] = joined
        fr[parity] = joined.astype(bf16)

    start(None, remote(fr.at[core], frp.at[core], fr_s.at[0], fr_r.at[core], "seq", partner))
    upper, lower = both(y == 1, has_up), both(y == 0, has_down)
    one, two = lax.rem(me + 1, n), lax.rem(me + 2, n)
    back, back2 = lax.rem(me + n - 1, n), lax.rem(me + n - 2, n)
    tail_rows, head_part = pl.ds(toks - HALO, HALO), pl.ds(0, HALO)
    for i, peer in enumerate((one, two)):
        for parity in (0, 1):
            start(upper, remote(fr.at[parity, tail_rows, :], halo_prev.at[parity],
                                halo_s.at[2 * i + parity], halo_r.at[parity], "seq", peer))
    for i, peer in enumerate((back, back2)):
        start(lower, remote(fr.at[0, head_part, :], halo_next,
                            halo_s.at[4 + i], halo_r.at[2], "seq", peer))
    for p in WQ_PIECES:
        push(None, p, me, 2, True)
    for p in W2_PIECES[2:]:
        relay(p, 1)

    for yy in (0, 1):
        @pl.when(y == yy)
        def _():
            for q in range(nz):
                dst = slice(q * depth, (q + 1) * depth)
                src = slice((2 * q + yy) * depth, (2 * q + yy + 1) * depth)
                w1h[:, dst] = w1_ref[:, src]
                b1h[0:1, dst] = vec_ref[0:1, src]
    for j in range(4):
        a, b = j * quarter, j * quarter + main2
        for r in (0, 1):
            gperm[r : r + 1, j * main2 : (j + 1) * main2] = vec_ref[1 + r : 2 + r, a:b]
            gperm[r : r + 1, rest_base + j * 64 : rest_base + (j + 1) * 64] = (
                vec_ref[1 + r : 2 + r, b : b + 64])

    first_token = lax.rem(me * toks, CONTEXT)
    lane = lax.broadcasted_iota(jnp.int32, (1, main2), 1)
    first_channel = lax.rem(h * quarter, half_width)

    def rate_of(channel):
        return jnp.exp(-(LOG_SCALE / (half_width - 1)) * (channel + first_channel).astype(f32))

    rate_main, rate_rest = rate_of(lane), rate_of(main2 + lax.rem(lane, 64))
    packed = ROWS + ROWS // 4

    def fill_place(wave):
        def step(i, c):
            token = first_token + i * ROWS + lax.broadcasted_iota(jnp.int32, (ROWS, 1), 0)
            token = jnp.where(token >= CONTEXT, token - CONTEXT, token)
            place[i, 0:ROWS, :] = wave(token.astype(f32) * rate_main)
            shape = (ROWS // 4, main2)
            token = (first_token + i * ROWS + lax.broadcasted_iota(jnp.int32, shape, 0)
                     + (ROWS // 4) * (lax.broadcasted_iota(jnp.int32, shape, 1) // 64))
            token = jnp.where(token >= CONTEXT, token - CONTEXT, token)
            place[i, ROWS:packed, :] = wave(token.astype(f32) * rate_rest)
            return c
        lax.fori_loop(0, chunks, step, 0)

    pl.when(h < 2)(lambda: fill_place(jnp.sin))
    pl.when(h >= 2)(lambda: fill_place(jnp.cos))

    for p in W2_PIECES[:2]:
        relay(p, 2)

    remote(fr.at[core], frp.at[core], fr_s.at[0], fr_r.at[core], "seq", partner).wait_recv()
    start(None, remote(frp.at[core], frp.at[core], fr_s.at[1], fr_r.at[core], "head", core_peer))
    remote(frp.at[1 - core], frp.at[1 - core], fr_s.at[1], fr_r.at[1 - core],
           "head", core_peer).wait_recv()
    for i in (0, 1):
        pl.when(has_down)(remote(halo_prev.at[i], halo_prev.at[i], halo_s.at[i], halo_r.at[i],
                                 "seq", partner).wait_recv)
    pl.when(has_up)(remote(halo_next, halo_next, halo_s.at[4], halo_r.at[2],
                           "seq", partner).wait_recv)
    ebuf[pl.ds(other, toks), :] = frp[0].astype(f32)
    obuf[pl.ds(other, toks), :] = frp[1].astype(f32)
    ebuf[0:HALO, :] = jnp.where(z > 0, halo_prev[0].astype(f32), 0.0)
    obuf[0:HALO, :] = jnp.where(z > 0, halo_prev[1].astype(f32), 0.0)
    ebuf[HALO + plane :, :] = jnp.where(z < nz - 1, halo_next[...].astype(f32), 0.0)
    x_even[:, 0:128] = obuf[HALO - 1 : HALO - 1 + plane, :].astype(bf16)
    x_even[:, 128:256] = ebuf[HALO : HALO + plane, :].astype(bf16)
    x_even[:, 256:384] = obuf[HALO : HALO + plane, :].astype(bf16)
    x_odd[:, 0:128] = ebuf[0 : HALO + plane, :].astype(bf16)
    x_odd[:, 128:256] = obuf[0 : HALO + plane, :].astype(bf16)
    x_odd[:, 256:384] = ebuf[1 : HALO + plane + 1, :].astype(bf16)

    tiles = [(a, min(a + 256, half_width)) for a in range(0, half_width, 256)]

    def first_conv(inputs, a, b):
        acc = jnp.dot(inputs, w1h[:, a:b], preferred_element_type=f32)
        return gelu(acc + b1h[0:1, a:b]).astype(bf16)

    def even_step(i, c):
        at = pl.ds(pl.multiple_of(i * toks, 16), toks)
        for a, b in tiles:
            f_mid[at, a:b] = first_conv(x_even[at, :], a, b)
        return c

    def odd_step(i, c):
        at = pl.multiple_of(i * toks, 16)
        for a, b in tiles:
            value = first_conv(x_odd[pl.ds(HALO + at, toks), :], a, b)
            f_mid[pl.ds(at, toks), half_width + a : half_width + b] = value
            f_odd[pl.ds(HALO + at, toks), a:b] = value
        return c

    lax.fori_loop(0, 2, even_step, 0)
    for p in W2_PIECES[2:]:
        relay(p, 2)
    for p in WQ_PIECES:
        own_along_z(p)
    lax.fori_loop(0, 2, odd_step, 0)
    for a, b in tiles:
        early = first_conv(x_odd[0:HALO, :], a, b)
        f_odd[0:HALO, a:b] = jnp.where(z > 0, early.astype(f32), 0.0).astype(bf16)
    for p in WQ_PIECES:
        relay_z(p, 1)

    for p in W2_PIECES:
        relay(p, 3)
    for p in W2_PIECES + WQ_PIECES:
        own_local(p).wait()
    for q in range(nz):
        for tap in (0, 1):
            at = tap * half_width + q * depth
            w2g[at : at + depth, main2:] = restg[q, 0:depth, 64 * tap : 64 * tap + 64]
        at = 2 * half_width + q * depth
        w2g[at : at + half, main2:] = restg[q, depth:, 0:64]
        w2g[at + half : at + depth, main2:] = restg[q, depth:, 64:128]

    odd_rows = (HALO + toks) // 3

    def partial_sums(slab, store):
        def tap_zero(i, c):
            at = pl.multiple_of(i * odd_rows, 16)
            acc0[pl.ds(at, odd_rows), :] = jnp.dot(
                f_odd[pl.ds(pl.multiple_of(slab * toks + at, 16), odd_rows), :],
                w2g[0:half_width, :], preferred_element_type=f32)
            return c

        lax.fori_loop(0, 3, tap_zero, 0)
        for i in range(chunks):
            at = pl.multiple_of(slab * toks + i * ROWS, ROWS)
            acc = jnp.dot(f_mid[pl.ds(at, ROWS), :], w2g[half_width:, :], preferred_element_type=f32)
            acc = acc + acc0[HALO - 1 + i * ROWS : HALO - 1 + (i + 1) * ROWS, :]
            store(i, acc)

    def store_packed(ref, i, acc):
        acc = acc.astype(ref.dtype)
        ref[i, 0:ROWS, :] = acc[:, 0:main2]
        step = ROWS // 4
        for b in range(4):
            ref[i, ROWS:packed, 64 * b : 64 * b + 64] = acc[b * step : (b + 1) * step, main2:]

    def send_partial(i, acc):
        store_packed(psend, i, acc)
        start(None, remote(psend.at[i], precv.at[i], p_s.at[i], p_r.at[i], "seq", partner))

    partial_sums(1 - y, send_partial)
    for p in WQ_PIECES:
        relay_z(p, 2)
    partial_sums(y, lambda i, acc: store_packed(accp, i, acc))

    bias_main = vec_ref[3:4, 0:main2]
    bias_rest = jnp.concatenate([vec_ref[3:4, main2:quarter]] * 4, axis=1)
    for i in range(chunks):
        remote(psend.at[i], precv.at[i], p_s.at[i], p_r.at[i], "seq", partner).wait_recv()
        for part, bias in ((slice(0, ROWS), bias_main), (slice(ROWS, packed), bias_rest)):
            value = accp[i, part, :] + precv[i, part, :].astype(f32) + bias
            stem[h, i, part, :] = (gelu(value) + place[i, part, :]).astype(bf16)
        mine = stem.at[h, i]
        start(None, remote(mine, mine, st_s.at[0, i], st_r.at[0, i], "head", x_peer))
        start(None, remote(mine, mine, st_s.at[1, i], st_r.at[1, i], "head", core_peer))

    for p in WQ_PIECES:
        relay_y(p, 1)
    for i in range(chunks):
        got = stem.at[x_peer, i]
        remote(got, got, st_s.at[0, i], st_r.at[0, i], "head", x_peer).wait_recv()
        start(None, remote(got, got, st_s.at[2, i], st_r.at[2, i], "head", core_peer))
    for i in range(chunks):
        got = stem.at[core_peer, i]
        remote(got, got, st_s.at[1, i], st_r.at[1, i], "head", core_peer).wait_recv()
        got = stem.at[far, i]
        remote(got, got, st_s.at[2, i], st_r.at[2, i], "head", core_peer).wait_recv()

    def normalise(i, c):
        step = ROWS // 4
        parts = [stem[j, i, 0:ROWS, :].astype(f32) for j in range(4)]
        tails = [stem[j, i, ROWS:packed, :].astype(f32) for j in range(4)]
        parts.append(jnp.concatenate(
            [jnp.concatenate([t[:, 64 * b : 64 * b + 64] for t in tails], axis=1) for b in range(4)],
            axis=0))
        mean = jnp.sum(sum(parts), axis=1, keepdims=True) / width_all
        parts = [v - mean for v in parts]
        var = jnp.sum(sum(v * v for v in parts), axis=1, keepdims=True) / width_all
        scale = lax.rsqrt(var + 1e-05)
        at = pl.ds(pl.multiple_of(i * ROWS, ROWS), ROWS)
        for j, v in enumerate(parts):
            lanes = slice(j * main2, (j + 1) * main2)
            nrm[at, lanes] = (v * scale * gperm[0:1, lanes] + gperm[1:2, lanes]).astype(bf16)
        return c

    lax.fori_loop(0, chunks, normalise, 0)
    for k in (2, 3):
        for p in WQ_PIECES:
            relay_y(p, k)
    for p in WQ_PIECES:
        for q in range(nz):
            arrive(None, p, 2 * q + (1 - y))
    for s in range(n):
        lo, hi = row_first(s), row_last(s)
        wqg[lo : lo + half, main_q:] = restqg[s, :, 0:64]
        wqg[lo + half : lo + first_q, main_q:] = restqg[s, 0 : first_q - half, 64:128]
        wqg[hi : hi + 64, main_q:] = restqg[s, first_q - half :, 64:128]

    def project(i, c):
        at = pl.ds(pl.multiple_of(i * 256, 256), 256)
        for a in range(0, out_cols, 256):
            b = min(a + 256, out_cols)
            out_ref[at, a:b] = jnp.dot(
                nrm[at, :], wqg[:, a:b], preferred_element_type=f32).astype(bf16)
        return c

    lax.fori_loop(0, toks // 256, project, 0)

    for cond, copy in pending:
        if cond is None:
            copy.wait_send()
        else:
            pl.when(cond)(copy.wait_send)


def fused_device(
    n, mel_buffer, segment_frames, conv1_weight, conv1_bias, conv2_weight, conv2_bias,
    norm_gain, norm_bias, qkv_weight,
):
    toks = mel_buffer.shape[0] // 4
    taps, mels, width_all = conv1_weight.shape
    depth, quarter = conv2_weight.shape[1:]
    out_cols = qkv_weight.shape[1]
    bf16, f32 = jnp.bfloat16, jnp.float32
    vec = jnp.zeros((), f32)
    rows_of = (conv1_bias, norm_gain, norm_bias, conv2_bias), (segment_frames.astype(f32),)
    for first, group in zip((0, 8), rows_of):
        for j, row in enumerate(group):
            vec = vec + jnp.pad(row[None, :], ((first + j, 15 - first - j), (0, width_all - row.shape[0])))
    vmem = pl.BlockSpec(memory_space=pltpu.VMEM)
    dma = pltpu.SemaphoreType.DMA
    plane, inner = 2 * toks, width_all // 2
    chunks, packed, main2 = toks // ROWS, ROWS + ROWS // 4, quarter - 64
    return pl.pallas_call(
        functools.partial(fused_kernel, (n, depth, width_all, quarter)),
        out_shape=jax.ShapeDtypeStruct((toks, out_cols), bf16),
        in_specs=[vmem] * 5,
        out_specs=vmem,
        scratch_shapes=[
            pltpu.VMEM((n, 8, 128), f32),
            pltpu.VMEM((toks, 128), bf16),
            pltpu.VMEM((2, toks, 128), bf16),
            pltpu.VMEM((2, toks, 128), bf16),
            pltpu.VMEM((2, toks, 128), bf16),
            pltpu.VMEM((2, HALO, 128), bf16),
            pltpu.VMEM((HALO, 128), bf16),
            pltpu.VMEM((plane + 2 * HALO, 128), f32),
            pltpu.VMEM((plane + 2 * HALO, 128), f32),
            pltpu.VMEM((plane, 384), bf16),
            pltpu.VMEM((plane + HALO, 384), bf16),
            pltpu.VMEM((taps * mels, inner), bf16),
            pltpu.VMEM((8, inner), f32),
            pltpu.VMEM((plane, width_all), bf16),
            pltpu.VMEM((plane + HALO, inner), bf16),
            pltpu.VMEM((3 * inner, quarter), bf16),
            pltpu.VMEM((width_all, out_cols), bf16),
            pltpu.VMEM((3 * depth // 2, 128), bf16),
            pltpu.VMEM((n // 2, 3 * depth // 2, 128), bf16),
            pltpu.VMEM((depth // 2, 128), bf16),
            pltpu.VMEM((n, depth // 2, 128), bf16),
            pltpu.VMEM((toks + HALO, quarter), f32),
            pltpu.VMEM((chunks, packed, main2), f32),
            pltpu.VMEM((chunks, packed, main2), bf16),
            pltpu.VMEM((chunks, packed, main2), bf16),
            pltpu.VMEM((chunks, packed, main2), f32),
            pltpu.VMEM((4, chunks, packed, main2), bf16),
            pltpu.VMEM((8, width_all), f32),
            pltpu.VMEM((toks, width_all), bf16),
            dma((n,)), dma((n,)), dma((2,)), dma((2,)), dma((2,)), dma((2,)), dma((6,)), dma((3,)),
            dma((7, n, 3)), dma((7, n)), dma((7,)), dma((chunks,)), dma((chunks,)),
            dma((3, chunks)), dma((3, chunks)),
        ],
        compiler_params=pltpu.CompilerParams(
            collective_id=0, has_side_effects=True, vmem_limit_bytes=60 * 1024 * 1024
        ),
    )(
        vec, mel_buffer, conv1_weight.reshape(taps * mels, width_all), conv2_weight, qkv_weight,
    )


def solution(mesh):
    n_seq, n_head = mesh.shape["seq"], mesh.shape["head"]

    def local(*args):
        depth, quarter = args[4].shape[1:]
        fits = n_head == 4 and n_seq == 8 and depth == 160 and quarter == 320
        if fits and args[0].shape[0] == 2048:
            return fused_device(n_seq, *args)
        return per_device(*args)

    in_specs = (
        P("seq", None),
        P("seq"),
        P(),
        P(),
        P(None, "seq", "head"),
        P("head"),
        P(),
        P(),
        P("seq", "head"),
    )
    out_specs = P("seq", "head")
    return jax.shard_map(
        local, mesh=mesh, in_specs=in_specs, out_specs=out_specs, check_vma=False
    )
```

time: 82.9 us -> 73.4 us (0.89)
  Pallas kernels: 77.6 us -> 67.7 us
    pallas_call x1, Pallas kernels: 77.6 us -> 67.7 us  [fused_device(): pl.pallas_call(functools.partial(fused_kernel, (n, depth, width_all, quar...]
where the time goes in v1:
time: 73.4 us; the launch traced here: 72.7 us
  Pallas kernels  67.7 us (92%)
  local copies, waits for them, and re-layouts  3.67 us (5%)
  other arithmetic  1.33 us (2%)
    pallas_call x1, Pallas kernels, fused_device(): pl.pallas_call(functools.partial(fused_kernel, (n, depth, width_all, quar...  67.7 us
    pallas_call x1, local copies, waits for them, and re-layouts, fused_device(): pl.pallas_call(functools.partial(fused_kernel, (n, depth, width_all, quar...  2.25 us

profile of v1, /device:TPU:0, one launch (start us, length us, event | category | flops | bytes accessed | tf_op | source)
XLA Modules:
  0.0 72.7 jit_solution(11677686749602551085)
XLA Ops:
  0.0 0.0 copy-start.2
  0.0 0.7 convert_bitcast_fusion
  0.7 0.0 copy-done.2
  0.7 0.0 copy-start
  0.7 0.7 broadcast_in_dim.15
  1.4 0.0 copy-done
  1.4 0.0 copy-start.1
  1.4 0.7 copy-done.1
  2.1 0.7 pad_add_fusion.vec_ref
  2.8 67.7 %shard_map.91 = bf16[512,960]{1,0:T(8,128)(2,1)} custom-call(f32[16,1280]{1,0:T(8,128)} %pad_add_fusion.vec_ref, bf16[2048,128]{1,0:T(8,128)(2,1)} %mel_ref.1, bf16[384,1280]{1,0:T(8,128)(2,1)} %bitcast.3, bf16[3,160,320]{2,1,0:T(8,128)(2,1)} %w2_ref.1, bf16[160,960]{1,0:T(8,128)(2,1)} %wq_ref.1), custom_call_target="tpu_custom_call" | custom-call | tf_op jit(solution)/shard_map/pallas_call | solution.py:593
  70.4 2.2 %copy.10 = bf16[512,960]{0,1:T(8,128)(2,1)} copy(bf16[512,960]{1,0:T(8,128)(2,1)} %shard_map.91) | data formatting | bytes 1966080 | tf_op jit(solution)/shard_map/pallas_call | solution.py:593
  (3 shorter events, 0.0 us)
Async XLA Ops:
  0.0 0.7 copy-start.2
  0.7 0.7 copy-start
  1.4 0.7 copy-start.1

commit v2 on v1

--- a/solution.py
+++ b/solution.py
@@ -141,8 +141,8 @@
 
 
 def fused_kernel(
-    dims, vec_ref, mel_ref, w1_ref, w2_ref, wq_ref,
-    out_ref, seg_all, tail_send, tail_recv, fr, frp, halo_prev, halo_next, ebuf, obuf, x_even, x_odd,
+    dims, seg_ref, b1_ref, b2_ref, gain_ref, shift_ref, mel_ref, w1_ref, w2_ref, wq_ref,
+    out_ref, vec_ref, seg_own, seg_all, tail_send, tail_recv, fr, frp, halo_prev, halo_next, ebuf, obuf, x_even, x_odd,
     w1h, b1h, f_mid, f_odd, w2g, wqg, rest, restg, restq, restqg, acc0, accp, psend, precv, place,
     stem, gperm, nrm, seg_s, seg_r, tail_s, tail_r, fr_s, fr_r, halo_s, halo_r,
     w_s, w_r, loc, p_s, p_r, st_s, st_r,
@@ -163,7 +163,6 @@
     core_peer = (h // 2) * 2 + (1 - core)
     x_peer = lax.rem(h + 2, 4)
     far = lax.rem(core_peer + 2, 4)
-    seg_ref = vec_ref.at[pl.ds(8, 8), pl.ds(0, 128)]
     pending = []
 
     def remote(src, dst, ss, rs, axis, peer):
@@ -195,9 +194,13 @@
         )
     pl.semaphore_wait(barrier, n - 1 + 3)
 
+    own_count = seg_ref[0]
+    for i in range(1, seg_ref.shape[0]):
+        own_count = own_count + seg_ref[i]
+    seg_own[...] = jnp.full(seg_own.shape, own_count, jnp.int32)
     for p in range(1, n):
         dst = lax.rem(me + p, n)
-        start(None, remote(seg_ref, seg_all.at[me], seg_s.at[p], seg_r.at[me], "seq", dst))
+        start(None, remote(seg_own, seg_all.at[me], seg_s.at[p], seg_r.at[me], "seq", dst))
 
     half = depth // 2
     out_cols = wqg.shape[1]
@@ -268,22 +271,35 @@
             arrive(valid, p, s)
             push(both(valid, onward), p, s, way)
 
-    def relay_z(p, k):
+    middle = both(has_up, has_down)
+    edge = jnp.logical_not(middle)
+
+    def arrivals(p, k, where):
+        for way in (0, 1):
+            valid, _, s = source(k, way)
+            arrive(both(valid, where), p, s)
+
+    def onward_z(p, k):
         for way in (0, 1):
             valid, onward, s = source(k, way)
-            arrive(both(valid, onward), p, s)
             push(both(valid, onward), p, s, way)
 
-    def relay_y(p, k):
+    def across_y(p, k, where, early=None):
         for way in (0, 1):
-            valid, onward, s = source(k, way)
-            arrive(both(valid, jnp.logical_not(onward)), p, s)
-            push(valid, p, s, 2)
-
-    own_along_z(2)
-    own_along_z(0)
-    restq[:, 0:64] = wq_ref[0:half, main_q:]
-    restq[:, 64:128] = wq_ref[half:, main_q:]
+            valid, _, s = source(k, way)
+            cond = both(valid, where)
+            if early is not None:
+                cond = both(cond, z % 2 == (1 - way if early else way))
+            push(cond, p, s, 2)
+
+    for p in WQ_PIECES:
+        if p == 6:
+            restq[:, 0:64] = wq_ref[0:half, main_q:]
+            restq[:, 64:128] = wq_ref[half:, main_q:]
+        if p == 4:
+            continue
+        push(None, p, me, 2, True)
+        own_along_z(p)
     rest[0:depth, 0:64] = w2_ref[0, :, main2:]
     rest[0:depth, 64:128] = w2_ref[1, :, main2:]
     rest[depth:, 0:64] = w2_ref[2, 0:half, main2:]
@@ -291,13 +307,16 @@
     for p in W2_PIECES + WQ_PIECES:
         own_local(p).start()
 
-    total = jnp.zeros((8, 128), f32)
+    for row, ref in enumerate((b1_ref, gain_ref, shift_ref, b2_ref)):
+        size = ref.shape[0]
+        vec_ref[row : row + 1, 0:size] = ref[...].reshape(1, size)
+
+    total = jnp.zeros((8, 128), jnp.int32)
     for p in range(1, n):
         src = lax.rem(me + n - p, n)
-        remote(seg_ref, seg_all.at[src], seg_s.at[p], seg_r.at[src], "seq", src).wait_recv()
-        total = total + jnp.where(src < me, seg_all[src], 0.0)
-    total = jnp.sum(jnp.sum(total, axis=1, keepdims=True), axis=0, keepdims=True)
-    moved = total.astype(jnp.int32) - me * frames_dev
+        remote(seg_own, seg_all.at[src], seg_s.at[p], seg_r.at[src], "seq", src).wait_recv()
+        total = total + jnp.where(src < me, seg_all[src], 0)
+    moved = total[0:1, 0:1] - me * frames_dev
 
     rows = ROWS
 
@@ -316,8 +335,13 @@
     tail = remote(tail_send, tail_recv.at[core], tail_s.at[0], tail_r.at[core],
                   "seq", lax.rem(me + 1, n))
     start(me < n - 1, tail)
-    own_along_z(1)
-    own_along_z(5)
+    push(None, 4, me, 2, True)
+    own_along_z(4)
+    for p in W2_PIECES:
+        own_along_z(p)
+    ebuf[0:HALO, :] = jnp.zeros((HALO, 128), f32)
+    obuf[0:HALO, :] = jnp.zeros((HALO, 128), f32)
+    ebuf[HALO + plane :, :] = jnp.zeros((HALO, 128), f32)
 
     base = pl.multiple_of(HALO + y * toks, 16)
     other = pl.multiple_of(HALO + (1 - y) * toks, 16)
@@ -355,10 +379,11 @@
     for i, peer in enumerate((back, back2)):
         start(lower, remote(fr.at[0, head_part, :], halo_next,
                             halo_s.at[4 + i], halo_r.at[2], "seq", peer))
-    for p in WQ_PIECES:
-        push(None, p, me, 2, True)
     for p in W2_PIECES[2:]:
         relay(p, 1)
+    for p in WQ_PIECES:
+        arrivals(p, 1, None)
+        across_y(p, 1, None, True)
 
     for yy in (0, 1):
         @pl.when(y == yy)
@@ -408,22 +433,14 @@
     start(None, remote(frp.at[core], frp.at[core], fr_s.at[1], fr_r.at[core], "head", core_peer))
     remote(frp.at[1 - core], frp.at[1 - core], fr_s.at[1], fr_r.at[1 - core],
            "head", core_peer).wait_recv()
-    for i in (0, 1):
-        pl.when(has_down)(remote(halo_prev.at[i], halo_prev.at[i], halo_s.at[i], halo_r.at[i],
-                                 "seq", partner).wait_recv)
-    pl.when(has_up)(remote(halo_next, halo_next, halo_s.at[4], halo_r.at[2],
-                           "seq", partner).wait_recv)
     ebuf[pl.ds(other, toks), :] = frp[0].astype(f32)
     obuf[pl.ds(other, toks), :] = frp[1].astype(f32)
-    ebuf[0:HALO, :] = jnp.where(z > 0, halo_prev[0].astype(f32), 0.0)
-    obuf[0:HALO, :] = jnp.where(z > 0, halo_prev[1].astype(f32), 0.0)
-    ebuf[HALO + plane :, :] = jnp.where(z < nz - 1, halo_next[...].astype(f32), 0.0)
     x_even[:, 0:128] = obuf[HALO - 1 : HALO - 1 + plane, :].astype(bf16)
     x_even[:, 128:256] = ebuf[HALO : HALO + plane, :].astype(bf16)
     x_even[:, 256:384] = obuf[HALO : HALO + plane, :].astype(bf16)
-    x_odd[:, 0:128] = ebuf[0 : HALO + plane, :].astype(bf16)
-    x_odd[:, 128:256] = obuf[0 : HALO + plane, :].astype(bf16)
-    x_odd[:, 256:384] = ebuf[1 : HALO + plane + 1, :].astype(bf16)
+    x_odd[HALO:, 0:128] = ebuf[HALO : HALO + plane, :].astype(bf16)
+    x_odd[HALO:, 128:256] = obuf[HALO : HALO + plane, :].astype(bf16)
+    x_odd[HALO:, 256:384] = ebuf[HALO + 1 : HALO + plane + 1, :].astype(bf16)
 
     tiles = [(a, min(a + 256, half_width)) for a in range(0, half_width, 256)]
 
@@ -449,13 +466,28 @@
     for p in W2_PIECES[2:]:
         relay(p, 2)
     for p in WQ_PIECES:
-        own_along_z(p)
+        onward_z(p, 1)
     lax.fori_loop(0, 2, odd_step, 0)
+    for i in (0, 1):
+        pl.when(has_down)(remote(halo_prev.at[i], halo_prev.at[i], halo_s.at[i], halo_r.at[i],
+                                 "seq", partner).wait_recv)
+    pl.when(has_up)(remote(halo_next, halo_next, halo_s.at[4], halo_r.at[2],
+                           "seq", partner).wait_recv)
+    ebuf[0:HALO, :] = jnp.where(z > 0, halo_prev[0].astype(f32), 0.0)
+    obuf[0:HALO, :] = jnp.where(z > 0, halo_prev[1].astype(f32), 0.0)
+    ebuf[HALO + plane :, :] = jnp.where(z < nz - 1, halo_next[...].astype(f32), 0.0)
+    x_even[0:HALO, 0:128] = obuf[HALO - 1 : 2 * HALO - 1, :].astype(bf16)
+    x_odd[0:HALO, 0:128] = ebuf[0:HALO, :].astype(bf16)
+    x_odd[0:HALO, 128:256] = obuf[0:HALO, :].astype(bf16)
+    x_odd[0:HALO, 256:384] = ebuf[1 : HALO + 1, :].astype(bf16)
+    x_odd[plane:, 256:384] = ebuf[plane + 1 : HALO + plane + 1, :].astype(bf16)
     for a, b in tiles:
         early = first_conv(x_odd[0:HALO, :], a, b)
         f_odd[0:HALO, a:b] = jnp.where(z > 0, early.astype(f32), 0.0).astype(bf16)
-    for p in WQ_PIECES:
-        relay_z(p, 1)
+        f_mid[0:HALO, a:b] = first_conv(x_even[0:HALO, :], a, b)
+        late = first_conv(x_odd[plane:, :], a, b)
+        f_odd[plane:, a:b] = late
+        f_mid[plane - HALO :, half_width + a : half_width + b] = late
 
     for p in W2_PIECES:
         relay(p, 3)
@@ -499,12 +531,20 @@
 
     partial_sums(1 - y, send_partial)
     for p in WQ_PIECES:
-        relay_z(p, 2)
+        across_y(p, 1, middle, False)
+    for p in WQ_PIECES:
+        arrivals(p, 2, middle)
+        onward_z(p, 2)
+        across_y(p, 2, middle)
     partial_sums(y, lambda i, acc: store_packed(accp, i, acc))
 
     bias_main = vec_ref[3:4, 0:main2]
     bias_rest = jnp.concatenate([vec_ref[3:4, main2:quarter]] * 4, axis=1)
     for i in range(chunks):
+        if i == chunks - 1:
+            for p in WQ_PIECES:
+                arrivals(p, 2, edge)
+                across_y(p, 2, edge)
         remote(psend.at[i], precv.at[i], p_s.at[i], p_r.at[i], "seq", partner).wait_recv()
         for part, bias in ((slice(0, ROWS), bias_main), (slice(ROWS, packed), bias_rest)):
             value = accp[i, part, :] + precv[i, part, :].astype(f32) + bias
@@ -513,8 +553,6 @@
         start(None, remote(mine, mine, st_s.at[0, i], st_r.at[0, i], "head", x_peer))
         start(None, remote(mine, mine, st_s.at[1, i], st_r.at[1, i], "head", core_peer))
 
-    for p in WQ_PIECES:
-        relay_y(p, 1)
     for i in range(chunks):
         got = stem.at[x_peer, i]
         remote(got, got, st_s.at[0, i], st_r.at[0, i], "head", x_peer).wait_recv()
@@ -542,10 +580,13 @@
             nrm[at, lanes] = (v * scale * gperm[0:1, lanes] + gperm[1:2, lanes]).astype(bf16)
         return c
 
+    for p in WQ_PIECES[:1]:
+        arrivals(p, 3, None)
+        across_y(p, 3, None)
     lax.fori_loop(0, chunks, normalise, 0)
-    for k in (2, 3):
-        for p in WQ_PIECES:
-            relay_y(p, k)
+    for p in WQ_PIECES[1:]:
+        arrivals(p, 3, None)
+        across_y(p, 3, None)
     for p in WQ_PIECES:
         for q in range(nz):
             arrive(None, p, 2 * q + (1 - y))
@@ -581,11 +622,6 @@
     depth, quarter = conv2_weight.shape[1:]
     out_cols = qkv_weight.shape[1]
     bf16, f32 = jnp.bfloat16, jnp.float32
-    vec = jnp.zeros((), f32)
-    rows_of = (conv1_bias, norm_gain, norm_bias, conv2_bias), (segment_frames.astype(f32),)
-    for first, group in zip((0, 8), rows_of):
-        for j, row in enumerate(group):
-            vec = vec + jnp.pad(row[None, :], ((first + j, 15 - first - j), (0, width_all - row.shape[0])))
     vmem = pl.BlockSpec(memory_space=pltpu.VMEM)
     dma = pltpu.SemaphoreType.DMA
     plane, inner = 2 * toks, width_all // 2
@@ -593,10 +629,12 @@
     return pl.pallas_call(
         functools.partial(fused_kernel, (n, depth, width_all, quarter)),
         out_shape=jax.ShapeDtypeStruct((toks, out_cols), bf16),
-        in_specs=[vmem] * 5,
+        in_specs=[pl.BlockSpec(memory_space=pltpu.SMEM)] + [vmem] * 8,
         out_specs=vmem,
         scratch_shapes=[
-            pltpu.VMEM((n, 8, 128), f32),
+            pltpu.VMEM((8, width_all), f32),
+            pltpu.VMEM((8, 128), jnp.int32),
+            pltpu.VMEM((n, 8, 128), jnp.int32),
             pltpu.VMEM((toks, 128), bf16),
             pltpu.VMEM((2, toks, 128), bf16),
             pltpu.VMEM((2, toks, 128), bf16),
@@ -633,7 +671,8 @@
             collective_id=0, has_side_effects=True, vmem_limit_bytes=60 * 1024 * 1024
         ),
     )(
-        vec, mel_buffer, conv1_weight.reshape(taps * mels, width_all), conv2_weight, qkv_weight,
+        segment_frames, conv1_bias, conv2_bias, norm_gain, norm_bias, mel_buffer,
+        conv1_weight.reshape(taps * mels, width_all), conv2_weight, qkv_weight,
     )
 
 

time: 73.4 us -> 68.2 us (0.929)
  Pallas kernels: 67.7 us -> 64.9 us
  local copies, waits for them, and re-layouts: 3.67 us -> 2.25 us
  other arithmetic: 1.33 us -> 0 us
    pallas_call x1, Pallas kernels: 67.7 us -> 64.9 us  [fused_device(): pl.pallas_call(functools.partial(fused_kernel, (n, depth, width_all, quar...]
where the time goes in v2:
time: 68.2 us; the launch traced here: 67.2 us
  Pallas kernels  64.9 us (95%)
  local copies, waits for them, and re-layouts  2.25 us (3%)
    pallas_call x1, Pallas kernels, fused_device(): pl.pallas_call(functools.partial(fused_kernel, (n, depth, width_all, quar...  64.9 us
    pallas_call x1, local copies, waits for them, and re-layouts, fused_device(): pl.pallas_call(functools.partial(fused_kernel, (n, depth, width_all, quar...  2.25 us

profile of v2, /device:TPU:0, one launch (start us, length us, event | category | flops | bytes accessed | tf_op | source)
XLA Modules:
  0.0 67.2 jit_solution(11170795625040122117)
XLA Ops:
  0.0 64.9 %shard_map.91 = bf16[512,960]{1,0:T(8,128)(2,1)} custom-call(s32[8]{0:T(128)} %seg_ref.1, f32[1280]{0:T(1024)} %b1_ref.1, f32[320]{0:T(512)} %b2_ref.1, f32[1280]{0:T(1024)} %gain_ref.1, f32[1280]{0:T(1024)} %shift_ref.1, bf16[2048,128]{1,0:T(8,128)(2,1)} %mel_ref.1, bf16[384,1280]{1,0:T(8,128)(2,1)} %bitcast.1, bf16[3,160,320]{2,1,0:T(8,128)(2,1)} %w2_ref.1, ...), custom_call_target="tpu_custom_call" | custom-call | tf_op jit(solution)/shard_map/pallas_call | solution.py:629
  64.9 2.2 %copy.10 = bf16[512,960]{0,1:T(8,128)(2,1)} copy(bf16[512,960]{1,0:T(8,128)(2,1)} %shard_map.91) | data formatting | bytes 1966080 | tf_op jit(solution)/shard_map/pallas_call | solution.py:629
